TPU v7x, 32 devices: a whole 2x2x4 slice. The times are simulated.
32 devices in a mesh: dp: 4 (over y, x), sp: 8 (over z, core).
Axes of the slice: x: 2, y: 2, z: 4, core: 2. Of those that a mesh axis runs over, the one named last changes fastest.
Arguments:
- first_layer_input: bfloat16 [8, 1024, 1024], P('dp', 'sp'), may hold values from -6 to 6
- cotangent: bfloat16 [8, 1024, 1024], P('dp', 'sp'), may hold values from -6 to 6
- document_begin: int32 [8, 1024], P('dp'), may hold values from 0 to 1023, as said below
- query_key_value_weight: bfloat16 [2, 1024, 3072], P(None, 'dp'), may hold values from -0.1875 to 0.1875
- attention_out_weight: bfloat16 [2, 1024, 1024], P(None, 'dp'), may hold values from -0.5 to 0.5
- feedforward_in_weight: bfloat16 [2, 1024, 4096], P(None, 'dp'), may hold values from -0.1875 to 0.1875
- feedforward_out_weight: bfloat16 [2, 4096, 1024], P(None, 'dp'), may hold values from -0.09375 to 0.09375
- query_value_bias: float32 [2, 2, 1024], replicated, may hold values from -3 to 3
- attention_out_bias: float32 [2, 1024], replicated, may hold values from -2 to 2
- feedforward_in_bias: float32 [2, 4096], replicated, may hold values from -2 to 2
- feedforward_out_bias: float32 [2, 1024], replicated, may hold values from -2 to 2
- layernorm_gain: float32 [2, 2, 1024], replicated, may hold values from 0.25 to 1.75
- layernorm_bias: float32 [2, 2, 1024], replicated, may hold values from -2 to 2
- adapter_down_maps: float32 [2, 2, 4, 1024], replicated, may hold values from -0.1875 to 0.1875
- adapter_up_maps: float32 [2, 2, 4, 1024], replicated, may hold values from -0.3 to 0.3
Outputs:
- output: float32 [8, 1024, 1024], P('dp', 'sp')
- input_grad: float32 [8, 1024, 1024], P('dp', 'sp')
- grad_down: float32 [2, 2, 4, 1024], replicated
- grad_up: float32 [2, 2, 4, 1024], replicated
Inputs may be any that keep to these rules, and one draw needn't show every extreme that they name: document_begin[s, t] is the first position of the document that holds token t of slot s: 0 at t = 0, never falling along a slot, equal to t where a document begins and constant inside a document. Of every aligned group of 2 slots, one is a single document; in every other slot the last token is a document of its own.
All inputs are finite; a program needn't handle non-finite values.
Results may differ from a plain program's by a relative error of at most 0.014.
Values may be sent and summed in bfloat16 or wider, within the bound.
A program may use at most 192 MiB of HBM per device.

v0:
```python
from functools import partial
import math
import jax
import jax.numpy as jnp
from jax import lax
from jax.sharding import PartitionSpec as P

HEAD_SIZE = 64
EPSILON = 1e-05
ADAPTER_ALPHA = 32.0
EXACT_PRECISION = lax.Precision.HIGHEST
MASKED = -1e30


def layer_norm(tensor, gains, shifts):
    row_mean = jnp.mean(tensor, -1, keepdims=True)
    centred = tensor - row_mean
    spread = jnp.mean(centred * centred, -1, keepdims=True)
    return centred * lax.rsqrt(spread + EPSILON) * gains + shifts


def fetch_weights(
    query_key_value_weight,
    attention_out_weight,
    feedforward_in_weight,
    feedforward_out_weight,
    layer_number,
):
    return (
        lax.all_gather(query_key_value_weight[layer_number], "dp", axis=0, tiled=True),
        lax.all_gather(attention_out_weight[layer_number], "dp", axis=0, tiled=True),
        lax.all_gather(feedforward_in_weight[layer_number], "dp", axis=0, tiled=True),
        lax.all_gather(feedforward_out_weight[layer_number], "dp", axis=0, tiled=True),
    )


def sum_adapters(down_terms, up_terms):
    return lax.psum((down_terms, up_terms), ("dp", "sp"))


def slot_scores(query_rows, key_rows, document_starts):
    length = query_rows.shape[0]
    heads_q = query_rows.reshape(length, -1, HEAD_SIZE)
    heads_k = key_rows.reshape(length, -1, HEAD_SIZE)
    scores = jnp.einsum("qhd,khd->hqk", heads_q, heads_k, preferred_element_type=jnp.float32)
    places = jnp.arange(length)
    allowed = (document_starts[:, None] == document_starts[None, :]) & (
        places[None, :] <= places[:, None]
    )
    return jnp.where(allowed[None], scores, MASKED)


def slot_forward(slot_items):
    query_rows, key_rows, value_rows, document_starts = slot_items
    length = query_rows.shape[0]
    scores = slot_scores(query_rows, key_rows, document_starts)
    row_max = jnp.max(scores, -1, keepdims=True)
    row_total = jnp.sum(jnp.exp(scores - row_max), -1, keepdims=True)
    log_total = row_max + jnp.log(row_total)
    probability = jnp.exp(scores - log_total).astype(jnp.bfloat16)
    mixture = jnp.einsum(
        "hqk,khd->qhd",
        probability,
        value_rows.reshape(length, -1, HEAD_SIZE),
        preferred_element_type=jnp.float32,
    )
    return (mixture.reshape(length, -1).astype(jnp.bfloat16), log_total[..., 0])


def slot_backward(slot_items):
    query_rows, key_rows, value_rows, document_starts, log_total, grad_mixture = slot_items
    length = query_rows.shape[0]
    scores = slot_scores(query_rows, key_rows, document_starts)
    probability = jnp.exp(scores - log_total[..., None])
    low_probability = probability.astype(jnp.bfloat16)
    grad_heads = grad_mixture.reshape(length, -1, HEAD_SIZE)
    value_heads = value_rows.reshape(length, -1, HEAD_SIZE)
    grad_values = jnp.einsum(
        "hqk,qhd->khd", low_probability, grad_heads, preferred_element_type=jnp.float32
    )
    grad_prob = jnp.einsum(
        "qhd,khd->hqk", grad_heads, value_heads, preferred_element_type=jnp.float32
    )
    grad_scores = probability * (grad_prob - jnp.sum(probability * grad_prob, -1, keepdims=True))
    low_scores = grad_scores.astype(jnp.bfloat16)
    grad_queries = jnp.einsum(
        "hqk,khd->qhd",
        low_scores,
        key_rows.reshape(length, -1, HEAD_SIZE),
        preferred_element_type=jnp.float32,
    )
    grad_keys = jnp.einsum(
        "hqk,qhd->khd",
        low_scores,
        query_rows.reshape(length, -1, HEAD_SIZE),
        preferred_element_type=jnp.float32,
    )
    return (
        grad_queries.reshape(length, -1).astype(jnp.bfloat16),
        grad_keys.reshape(length, -1).astype(jnp.bfloat16),
        grad_values.reshape(length, -1).astype(jnp.bfloat16),
    )


def layer_forward(hidden_state, weight_set, params, document_begin):
    query_key_value_weight, attention_out_weight, feedforward_in_weight, feedforward_out_weight = (
        weight_set
    )
    (
        query_value_bias,
        attention_out_bias,
        feedforward_in_bias,
        feedforward_out_bias,
        gains,
        shifts,
        down_projection,
        up_projection,
    ) = params
    model_dimension = hidden_state.shape[-1]
    normed = layer_norm(hidden_state, gains[0], shifts[0]).astype(jnp.bfloat16)
    projected_rows = jnp.einsum(
        "std,de->ste", normed, query_key_value_weight, preferred_element_type=jnp.float32
    )
    widened = normed.astype(jnp.float32)
    adapter_scale = ADAPTER_ALPHA / down_projection.shape[1]
    query_row_block = jnp.einsum(
        "nyh,lh->nyl", widened, down_projection[0], precision=EXACT_PRECISION
    )
    value_row_block = jnp.einsum(
        "nyh,lh->nyl", widened, down_projection[1], precision=EXACT_PRECISION
    )
    query_rows = (
        (
            projected_rows[..., :model_dimension]
            + query_value_bias[0]
            + adapter_scale
            * jnp.einsum(
                "wah,hp->wap", query_row_block, up_projection[0], precision=EXACT_PRECISION
            )
        )
        * HEAD_SIZE ** (-0.5)
    ).astype(jnp.bfloat16)
    key_rows = projected_rows[..., model_dimension : 2 * model_dimension].astype(jnp.bfloat16)
    value_rows = (
        projected_rows[..., 2 * model_dimension :]
        + query_value_bias[1]
        + adapter_scale
        * jnp.einsum("wah,hp->wap", value_row_block, up_projection[1], precision=EXACT_PRECISION)
    ).astype(jnp.bfloat16)
    queries_h, keys_h, values_h = (
        lax.all_to_all(query_rows, "sp", split_axis=2, concat_axis=1, tiled=True),
        lax.all_to_all(key_rows, "sp", split_axis=2, concat_axis=1, tiled=True),
        lax.all_to_all(value_rows, "sp", split_axis=2, concat_axis=1, tiled=True),
    )
    mixture_h, log_total = lax.map(slot_forward, (queries_h, keys_h, values_h, document_begin))
    mixture = lax.all_to_all(mixture_h, "sp", split_axis=1, concat_axis=2, tiled=True)
    attended = hidden_state + (
        jnp.einsum("std,de->ste", mixture, attention_out_weight, preferred_element_type=jnp.float32)
        + attention_out_bias
    )
    normed_mlp = layer_norm(attended, gains[1], shifts[1]).astype(jnp.bfloat16)
    pre_act = (
        jnp.einsum(
            "std,df->stf", normed_mlp, feedforward_in_weight, preferred_element_type=jnp.float32
        )
        + feedforward_in_bias
    )
    activation = jax.nn.gelu(pre_act, approximate=True).astype(jnp.bfloat16)
    final_result = attended + (
        jnp.einsum(
            "stf,fd->std", activation, feedforward_out_weight, preferred_element_type=jnp.float32
        )
        + feedforward_out_bias
    )
    saved_state = (
        normed,
        query_row_block,
        value_row_block,
        queries_h,
        keys_h,
        values_h,
        log_total,
        attended,
        pre_act,
    )
    return (final_result, saved_state)


def layer_backward(hidden_state, gradient, weight_set, params, document_begin, saved_state):
    query_key_value_weight, attention_out_weight, feedforward_in_weight, feedforward_out_weight = (
        weight_set
    )
    (
        query_value_bias,
        attention_out_bias,
        feedforward_in_bias,
        feedforward_out_bias,
        gains,
        shifts,
        down_projection,
        up_projection,
    ) = params
    (
        normed,
        query_row_block,
        value_row_block,
        queries_h,
        keys_h,
        values_h,
        log_total,
        attended,
        pre_act,
    ) = saved_state
    grad_act = jnp.einsum(
        "std,fd->stf",
        gradient.astype(jnp.bfloat16),
        feedforward_out_weight,
        preferred_element_type=jnp.float32,
    )
    unused_act, gelu_back = jax.vjp(partial(jax.nn.gelu, approximate=True), pre_act)
    grad_pre = gelu_back(grad_act)[0].astype(jnp.bfloat16)
    grad_normed_mlp = jnp.einsum(
        "stf,df->std", grad_pre, feedforward_in_weight, preferred_element_type=jnp.float32
    )
    unused_norm, second_back = jax.vjp(
        lambda tensor: layer_norm(tensor, gains[1], shifts[1]), attended
    )
    grad_attended = gradient + second_back(grad_normed_mlp)[0]
    grad_mixture = jnp.einsum(
        "ste,de->std",
        grad_attended.astype(jnp.bfloat16),
        attention_out_weight,
        preferred_element_type=jnp.float32,
    ).astype(jnp.bfloat16)
    grad_mixture_h = lax.all_to_all(grad_mixture, "sp", split_axis=2, concat_axis=1, tiled=True)
    grad_q_h, grad_k_h, grad_v_h = lax.map(
        slot_backward, (queries_h, keys_h, values_h, document_begin, log_total, grad_mixture_h)
    )
    grad_queries, grad_keys, grad_values = (
        lax.all_to_all(grad_q_h, "sp", split_axis=1, concat_axis=2, tiled=True),
        lax.all_to_all(grad_k_h, "sp", split_axis=1, concat_axis=2, tiled=True),
        lax.all_to_all(grad_v_h, "sp", split_axis=1, concat_axis=2, tiled=True),
    )
    grad_queries = grad_queries * jnp.asarray(HEAD_SIZE ** (-0.5), jnp.bfloat16)
    stacked = jnp.concatenate([grad_queries, grad_keys, grad_values], -1)
    grad_normed = jnp.einsum(
        "ste,de->std", stacked, query_key_value_weight, preferred_element_type=jnp.float32
    )
    adapter_scale = ADAPTER_ALPHA / down_projection.shape[1]
    widened = normed.astype(jnp.float32)
    query_widened = grad_queries.astype(jnp.float32)
    value_widened = grad_values.astype(jnp.float32)
    query_row_gradient = adapter_scale * jnp.einsum(
        "nyh,lh->nyl", query_widened, up_projection[0], precision=EXACT_PRECISION
    )
    value_row_gradient = adapter_scale * jnp.einsum(
        "nyh,lh->nyl", value_widened, up_projection[1], precision=EXACT_PRECISION
    )
    query_up_weight = adapter_scale * jnp.einsum(
        "fkp,fkz->pz", query_row_block, query_widened, precision=EXACT_PRECISION
    )
    value_up_weight = adapter_scale * jnp.einsum(
        "fkp,fkz->pz", value_row_block, value_widened, precision=EXACT_PRECISION
    )
    down_q = jnp.einsum("fkp,fkz->pz", query_row_gradient, widened, precision=EXACT_PRECISION)
    down_v = jnp.einsum("fkp,fkz->pz", value_row_gradient, widened, precision=EXACT_PRECISION)
    grad_normed = (
        grad_normed
        + jnp.einsum(
            "wah,hp->wap", query_row_gradient, down_projection[0], precision=EXACT_PRECISION
        )
        + jnp.einsum(
            "wah,hp->wap", value_row_gradient, down_projection[1], precision=EXACT_PRECISION
        )
    )
    unused_first, first_back = jax.vjp(
        lambda tensor: layer_norm(tensor, gains[0], shifts[0]), hidden_state
    )
    grad_hidden = grad_attended + first_back(grad_normed)[0]
    return (grad_hidden, jnp.stack([down_q, down_v]), jnp.stack([query_up_weight, value_up_weight]))


def body(
    first_layer_input,
    cotangent,
    document_begin,
    query_key_value_weight,
    attention_out_weight,
    feedforward_in_weight,
    feedforward_out_weight,
    query_value_bias,
    attention_out_bias,
    feedforward_in_bias,
    feedforward_out_bias,
    layernorm_gain,
    layernorm_bias,
    adapter_down_maps,
    adapter_up_maps,
):
    layers = query_key_value_weight.shape[0]

    def params_of(layer_number):
        return (
            query_value_bias[layer_number],
            attention_out_bias[layer_number],
            feedforward_in_bias[layer_number],
            feedforward_out_bias[layer_number],
            layernorm_gain[layer_number],
            layernorm_bias[layer_number],
            adapter_down_maps[layer_number],
            adapter_up_maps[layer_number],
        )

    hidden_state = first_layer_input.astype(jnp.float32)
    inputs = []
    gathered = []
    for layer_number in range(layers):
        weight_set = fetch_weights(
            query_key_value_weight,
            attention_out_weight,
            feedforward_in_weight,
            feedforward_out_weight,
            layer_number,
        )
        inputs.append(hidden_state)
        gathered.append(weight_set)
        hidden_state, unused_state = layer_forward(
            hidden_state, weight_set, params_of(layer_number), document_begin
        )
    gradient = cotangent.astype(jnp.float32)
    down_parts = [None] * layers
    up_parts = [None] * layers
    for layer_number in reversed(range(layers)):
        weight_set = fetch_weights(
            query_key_value_weight,
            attention_out_weight,
            feedforward_in_weight,
            feedforward_out_weight,
            layer_number,
        )
        unused_result, saved_state = layer_forward(
            inputs[layer_number], weight_set, params_of(layer_number), document_begin
        )
        gradient, down_terms, up_terms = layer_backward(
            inputs[layer_number],
            gradient,
            weight_set,
            params_of(layer_number),
            document_begin,
            saved_state,
        )
        down_parts[layer_number] = down_terms
        up_parts[layer_number] = up_terms
    grad_down = jnp.stack(down_parts)
    grad_up = jnp.stack(up_parts)
    grad_down, grad_up = sum_adapters(grad_down, grad_up)
    tokens = (
        first_layer_input.shape[0]
        * first_layer_input.shape[1]
        * lax.axis_size("dp")
        * lax.axis_size("sp")
    )
    token_scale = 1.0 / math.sqrt(tokens)
    return (hidden_state, gradient, grad_down * token_scale, grad_up * token_scale)


def solution(mesh):
    placed = (
        P("dp", "sp", None),
        P("dp", "sp", None),
        P("dp", None),
        P(None, "dp", None),
        P(None, "dp", None),
        P(None, "dp", None),
        P(None, "dp", None),
        P(),
        P(),
        P(),
        P(),
        P(),
        P(),
        P(),
        P(),
    )
    return jax.shard_map(
        body,
        mesh=mesh,
        in_specs=placed,
        out_specs=(P("dp", "sp", None), P("dp", "sp", None), P(), P()),
        check_vma=False,
    )
```

profile of v0, /device:TPU:0, one launch (start us, length us, event | category | flops | bytes accessed | tf_op | source)
XLA Modules:
  0.0 1025.3 jit_solution(3215920100778661397)
XLA Ops:
  25.0 59.0 %all-gather.17.cloned.1.call-done = bf16[1,1024,3072]{2,1,0:T(8,128)(2,1)} async-done(((bf16[1,256,3072]{2,1,0:T(8,128)(2,1)}), bf16[1,1024,3072]{2,1,0:T(8,128)(2,1)}) %all-gather.17.cloned.1.call-update) | async-done | bytes 6291472 | tf_op jit(solution)/shard_map/all_gather | solution.py:30
  101.4 11.2 %all-to-all-done = bf16[2,128,1024]{1,0,2:T(2,128)(2,1)S(1)} async-done(((bf16[2,128,1024]{1,0,2:T(2,128)(2,1)}), bf16[2,128,1024]{1,0,2:T(2,128)(2,1)S(1)}, u32[]{:S(2)}, u32[]{:S(2)}) %all-to-all-start) | async-done | bytes 524320 | tf_op jit(solution)/shard_map/all_to_all | solution.py:153
  118.6 12.9 %all-to-all-done.1 = bf16[2,128,1024]{1,0,2:T(2,128)(2,1)S(1)} async-done(((bf16[2,128,1024]{1,0,2:T(2,128)(2,1)}), bf16[2,128,1024]{1,0,2:T(2,128)(2,1)S(1)}, u32[]{:S(2)}, u32[]{:S(2)}) %all-to-all-start.1) | async-done | bytes 524320 | tf_op jit(solution)/shard_map/all_to_all | solution.py:151
  136.9 13.3 %all-to-all-done.2 = bf16[2,128,1024]{1,0,2:T(2,128)(2,1)S(1)} async-done(((bf16[2,128,1024]{1,0,2:T(2,128)(2,1)}), bf16[2,128,1024]{1,0,2:T(2,128)(2,1)S(1)}, u32[]{:S(2)}, u32[]{:S(2)}) %all-to-all-start.2) | async-done | bytes 524320 | tf_op jit(solution)/shard_map/all_to_all | solution.py:152
  150.9 12.9 %while.72 = (s32[]{:T(128)}, bf16[2,1024,128]{1,2,0:T(8,128)(2,1)S(1)}, bf16[2,1024,128]{1,2,0:T(8,128)(2,1)S(1)}, s32[2,1024]{1,0:T(2,128)S(1)}, bf16[2,1024,12...) while((s32[]{:T(128)}, bf16[2,1024,128]{1,2,0:T(8,128)(2,1)S(1)}, ...), condition=%wide.region_5.6_spmd, body=%wide.region_2.5_spmd.sunk | while | flops 556922880 | bytes 32575588 | solution.py:155
  169.3 14.6 %all-to-all-done.3 = bf16[2,1024,128]{2,0,1:T(2,128)(2,1)S(1)} async-done(((bf16[2,1024,128]{2,0,1:T(2,128)(2,1)}), bf16[2,1024,128]{2,0,1:T(2,128)(2,1)S(1)}, u32[]{:S(2)}, u32[]{:S(2)}) %all-to-all-start.3) | async-done | bytes 524320 | tf_op jit(solution)/shard_map/all_to_all | solution.py:156
  188.2 22.6 %all-gather.23.cloned.1.call-done = bf16[1,4096,1024]{2,1,0:T(8,128)(2,1)} async-done(((bf16[1,1024,1024]{2,1,0:T(8,128)(2,1)}), bf16[1,4096,1024]{2,1,0:T(8,128)(2,1)}) %all-gather.23.cloned.1.call-update) | async-done | bytes 8388624 | tf_op jit(solution)/shard_map/all_gather | solution.py:33
  210.8 89.3 %all-gather.21.cloned.1.call-done = bf16[1,1024,4096]{2,1,0:T(8,128)(2,1)} async-done(((bf16[1,256,4096]{2,1,0:T(8,128)(2,1)}), bf16[1,1024,4096]{2,1,0:T(8,128)(2,1)}) %all-gather.21.cloned.1.call-update) | async-done | bytes 8388624 | tf_op jit(solution)/shard_map/all_gather | solution.py:32
  300.1 11.5 %fusion.337 = (f32[2,128]{1,0:T(2,128)S(1)}, f32[2,128,1024]{2,1,0:T(8,128)S(1)}) fusion(f32[2,128,1024]{2,1,0:T(8,128)} %copy-done.51, f32[1024]{0:T(1024)S(1)} %bitcast.735, bf16[1,4096,1024]{2,1,0:T(8,128)(2,1)} %all-gather.23.cloned.1.call-done, bf16[1,1024,4096]{2,1,0:T(8,128)(2,1)} %all-gather.21.cloned.1.call-done, f32[4096]{0:T(1024)S(1)} %bitcast.730, ...), kind=kOutput, calls=%fused_computation.425 | convolution fusion | flops 4307550208 | bytes 18906112 | tf_op jit(solution)/shard_map/stf,fd->std/dot_general | solution.py:170
  313.4 58.7 %all-gather.25.cloned.1.call-done = bf16[1,1024,3072]{2,1,0:T(8,128)(2,1)} async-done(((bf16[1,256,3072]{2,1,0:T(8,128)(2,1)}), bf16[1,1024,3072]{2,1,0:T(8,128)(2,1)}) %all-gather.25.cloned.1.call-update) | async-done | bytes 6291472 | tf_op jit(solution)/shard_map/all_gather | solution.py:30
  409.8 11.2 %all-to-all-done.5 = bf16[2,128,1024]{1,0,2:T(2,128)(2,1)S(1)} async-done(((bf16[2,128,1024]{1,0,2:T(2,128)(2,1)}), bf16[2,128,1024]{1,0,2:T(2,128)(2,1)S(1)}, u32[]{:S(2)}, u32[]{:S(2)}) %all-to-all-start.5) | async-done | bytes 524320 | tf_op jit(solution)/shard_map/all_to_all | solution.py:151
  446.1 16.5 %while.74 = (s32[]{:T(128)}, bf16[2,1024,128]{1,2,0:T(8,128)(2,1)}, f32[2,2,1024]{2,1,0:T(2,128)S(1)}, bf16[2,1024,128]{1,2,0:T(8,128)(2,1)S(1)}, s32[2,1024]{1,...) while((s32[]{:T(128)}, bf16[2,1024,128]{1,2,0:T(8,128)(2,1)}, ...), condition=%wide.region_19.20_spmd, body=%wide.region_16.19_spmd.sunk | while | flops 556922880 | bytes 36778152 | solution.py:155
  468.9 15.4 %all-to-all-done.8 = bf16[2,1024,128]{2,0,1:T(2,128)(2,1)} async-done(((bf16[2,1024,128]{2,0,1:T(2,128)(2,1)}), bf16[2,1024,128]{2,0,1:T(2,128)(2,1)}, u32[]{:S(2)}, u32[]{:S(2)}) %all-to-all-start.8) | async-done | bytes 524320 | tf_op jit(solution)/shard_map/all_to_all | solution.py:156
  507.1 81.4 %all-gather.31.cloned.1.call-done = bf16[1,4096,1024]{2,1,0:T(8,128)(2,1)} async-done(((bf16[1,1024,1024]{2,1,0:T(8,128)(2,1)}), bf16[1,4096,1024]{2,1,0:T(8,128)(2,1)}) %all-gather.31.cloned.1.call-update) | async-done | bytes 8388624 | tf_op jit(solution)/shard_map/all_gather | solution.py:33
  588.5 12.2 %multiply_reduce_fusion.5 = (f32[2,128]{1,0:T(2,128)S(1)}, f32[2,128,1024]{2,1,0:T(8,128)}) fusion(f32[2,128,1024]{2,1,0:T(8,128)S(1)} %copy-done.22, f32[2,128]{1,0:T(2,128)S(1)} %broadcast_multiply_fusion.5, f32[1024]{0:T(1024)S(1)} %bitcast.744, bf16[1,1024,4096]{2,1,0:T(8,128)(2,1)} %all-gather.29.cloned.1.call-done, f32[2,128,4096]{2,1,0:T(8,128)} %fusion.75, ...), kind=kOutput, calls=%fused_computation.279 | convolution fusion | flops 4316987392 | bytes 23599104 | tf_op jit(solution)/shard_map/stf,df->std/dot_general | solution.py:222
  613.3 15.4 %while.76 = (s32[]{:T(128)}, bf16[2,1024,128]{1,2,0:T(8,128)(2,1)}, f32[2,2,1024]{2,1,0:T(2,128)}, bf16[2,1024,128]{1,2,0:T(8,128)(2,1)S(1)}, s32[2,1024]{1,0:T(...) while((s32[]{:T(128)}, bf16[2,1024,128]{1,2,0:T(8,128)(2,1)}, ...), condition=%wide.region_32.33_spmd, body=%wide.region_29.32_spmd.sunk | while | flops 556922880 | bytes 32583792 | solution.py:155
  643.3 27.2 %while.75 = (s32[]{:T(128)}, bf16[2,1024,128]{1,2,0:T(8,128)(2,1)}, bf16[2,1024,128]{1,2,0:T(8,128)(2,1)}, bf16[2,1024,128]{1,2,0:T(8,128)(2,1)}, bf16[2,1024,12...) while((s32[]{:T(128)}, bf16[2,1024,128]{1,2,0:T(8,128)(2,1)}, ...), condition=%wide.region_26.27_spmd, body=%wide.region_24.26_spmd.sunk | while | flops 1370880000 | bytes 88150360 | solution.py:236
  716.0 12.9 %while.73 = (s32[]{:T(128)}, bf16[2,1024,128]{1,2,0:T(8,128)(2,1)S(1)}, bf16[2,1024,128]{1,2,0:T(8,128)(2,1)S(1)}, s32[2,1024]{1,0:T(2,128)S(1)}, bf16[2,1024,12...) while((s32[]{:T(128)}, bf16[2,1024,128]{1,2,0:T(8,128)(2,1)S(1)}, ...), condition=%wide.region_13.14_spmd, body=%wide.region_10.13_spmd.sunk | while | flops 556922880 | bytes 32575588 | solution.py:155
  749.0 11.9 %multiply_reduce_fusion.2 = (f32[2,128]{1,0:T(2,128)S(1)}, f32[2,128,1024]{2,1,0:T(8,128)}) fusion(f32[2,128,1024]{2,1,0:T(8,128)S(1)} %copy-done.29, f32[2,128]{1,0:T(2,128)S(1)} %broadcast_multiply_fusion.4, f32[1024]{0:T(1024)S(1)} %bitcast.748, bf16[1,1024,4096]{2,1,0:T(8,128)(2,1)} %all-gather.21.cloned.1.call-done, f32[2,128,4096]{2,1,0:T(8,128)} %fusion.69, ...), kind=kOutput, calls=%fused_computation.273 | convolution fusion | flops 4317249536 | bytes 24123392 | tf_op jit(solution)/shard_map/stf,df->std/dot_general | solution.py:222
  792.7 28.4 %while.77 = (s32[]{:T(128)}, bf16[2,1024,128]{1,2,0:T(8,128)(2,1)}, bf16[2,1024,128]{1,2,0:T(8,128)(2,1)}, bf16[2,1024,128]{1,2,0:T(8,128)(2,1)}, bf16[2,1024,12...) while((s32[]{:T(128)}, bf16[2,1024,128]{1,2,0:T(8,128)(2,1)}, ...), condition=%wide.region_39.40_spmd, body=%wide.region_37.39_spmd.sunk | while | flops 1370880000 | bytes 86053176 | solution.py:236
  830.7 11.2 %all-to-all-done.17 = bf16[2,1024,128]{2,0,1:T(2,128)(2,1)S(1)} async-done(((bf16[2,1024,128]{2,0,1:T(2,128)(2,1)}), bf16[2,1024,128]{2,0,1:T(2,128)(2,1)S(1)}, u32[]{:S(2)}, u32[]{:S(2)}) %all-to-all-start.17) | async-done | bytes 524320 | tf_op jit(solution)/shard_map/all_to_all | solution.py:242
  846.5 12.0 %fusion.191 = f32[2,128,1024]{2,1,0:T(8,128)} fusion(f32[2,128,1024]{2,1,0:T(8,128)S(1)} %get-tuple-element.421, bf16[1,4096,1024]{2,1,0:T(8,128)(2,1)} %all-gather.31.cloned.1.call-done, bf16[1,1024,4096]{2,1,0:T(8,128)(2,1)} %all-gather.29.cloned.1.call-done, f32[4096]{0:T(1024)S(1)} %bitcast.729, f32[1024]{0:T(1024)S(1)} %bitcast.732, ...), kind=kOutput, calls=%fused_computation.233 | convolution fusion | flops 4307288064 | bytes 18905088 | tf_op jit(solution)/shard_map/stf,fd->std/dot_general | solution.py:170
  871.8 11.3 %all-to-all-done.16 = bf16[2,1024,128]{2,0,1:T(2,128)(2,1)S(1)} async-done(((bf16[2,1024,128]{2,0,1:T(2,128)(2,1)}), bf16[2,1024,128]{2,0,1:T(2,128)(2,1)S(1)}, u32[]{:S(2)}, u32[]{:S(2)}) %all-to-all-start.16) | async-done | bytes 524320 | tf_op jit(solution)/shard_map/all_to_all | solution.py:241
  897.1 118.2 %all-reduce.3.cloned.1.call-done = (f32[2,2,4,1024]{3,2,1,0:T(4,128)}, f32[2,2,4,1024]{3,2,1,0:T(4,128)}) async-done(((f32[2,2,4,1024]{3,2,1,0:T(4,128)}, f32[2,2,4,1024]{3,2,1,0:T(4,128)}), (f32[2,2,4,1024]{3,2,1,0:T(4,128)}, f32[2,2,4,1024]{3,2,1,0:T(4,128)})) %all-reduce.3.cloned.1.call-update) | async-done | bytes 131088 | tf_op jit(solution)/shard_map/psum | solution.py:38
  (595 shorter events, 430.2 us)
Async XLA Ops:
  7.2 76.9 %all-gather.17.cloned.1.call-start = ((), (), s32[]{:S(2)}) async-start(), calls=%async_computation.18 | async-start | bytes 7864320 | tf_op jit(solution)/shard_map/all_gather | solution.py:30
  11.0 174.3 %all-gather.19.cloned.1.call-start = ((), (), s32[]{:S(2)}) async-start(), calls=%async_computation.19 | async-start | bytes 2621440 | tf_op jit(solution)/shard_map/all_gather | solution.py:31
  12.1 198.7 %all-gather.23.cloned.1.call-start = ((), (), s32[]{:S(2)}) async-start(), calls=%async_computation.21 | async-start | bytes 10485760 | tf_op jit(solution)/shard_map/all_gather | solution.py:33
  16.8 283.3 %all-gather.21.cloned.1.call-start = ((), (), s32[]{:S(2)}) async-start(), calls=%async_computation.20 | async-start | bytes 10485760 | tf_op jit(solution)/shard_map/all_gather | solution.py:32
  21.8 350.3 %all-gather.25.cloned.1.call-start = ((), (), s32[]{:S(2)}) async-start(), calls=%async_computation.22 | async-start | bytes 7864320 | tf_op jit(solution)/shard_map/all_gather | solution.py:30
  22.4 466.1 %all-gather.27.cloned.1.call-start = ((), (), s32[]{:S(2)}) async-start(), calls=%async_computation.23 | async-start | bytes 2621440 | tf_op jit(solution)/shard_map/all_gather | solution.py:31
  22.9 476.0 %all-gather.29.cloned.1.call-start = ((), (), s32[]{:S(2)}) async-start(), calls=%async_computation.24 | async-start | bytes 10485760 | tf_op jit(solution)/shard_map/all_gather | solution.py:32
  92.7 20.0 %all-to-all-start = ((bf16[2,128,1024]{1,0,2:T(2,128)(2,1)}), bf16[2,128,1024]{1,0,2:T(2,128)(2,1)S(1)}, u32[]{:S(2)}, u32[]{:S(2)}) async-start(bf16[2,128,1024]{1,0,2:T(2,128)(2,1)} %copy.57), calls=%async_computation | async-start | bytes 1048576 | tf_op jit(solution)/shard_map/all_to_all | solution.py:153
  131.4 18.8 %all-to-all-start.2 = ((bf16[2,128,1024]{1,0,2:T(2,128)(2,1)}), bf16[2,128,1024]{1,0,2:T(2,128)(2,1)S(1)}, u32[]{:S(2)}, u32[]{:S(2)}) async-start(bf16[2,128,1024]{1,0,2:T(2,128)(2,1)} %copy.61), calls=%async_computation.2 | async-start | bytes 1048576 | tf_op jit(solution)/shard_map/all_to_all | solution.py:152
  135.0 453.5 %all-gather.31.cloned.1.call-start = ((), (), s32[]{:S(2)}) async-start(), calls=%async_computation.25 | async-start | bytes 10485760 | tf_op jit(solution)/shard_map/all_gather | solution.py:33
  164.9 19.0 %all-to-all-start.3 = ((bf16[2,1024,128]{2,0,1:T(2,128)(2,1)}), bf16[2,1024,128]{2,0,1:T(2,128)(2,1)S(1)}, u32[]{:S(2)}, u32[]{:S(2)}) async-start(bf16[2,1024,128]{2,0,1:T(2,128)(2,1)} %copy.63), calls=%async_computation.3 | async-start | bytes 1048576 | tf_op jit(solution)/shard_map/all_to_all | solution.py:156
  382.1 20.1 %all-to-all-start.4 = ((bf16[2,128,1024]{1,0,2:T(2,128)(2,1)}), bf16[2,128,1024]{1,0,2:T(2,128)(2,1)}, u32[]{:S(2)}, u32[]{:S(2)}) async-start(bf16[2,128,1024]{1,0,2:T(2,128)(2,1)} %copy.65), calls=%async_computation.4 | async-start | bytes 1048576 | tf_op jit(solution)/shard_map/all_to_all | solution.py:153
  421.0 20.0 %all-to-all-start.6 = ((bf16[2,128,1024]{1,0,2:T(2,128)(2,1)}), bf16[2,128,1024]{1,0,2:T(2,128)(2,1)}, u32[]{:S(2)}, u32[]{:S(2)}) async-start(bf16[2,128,1024]{1,0,2:T(2,128)(2,1)} %copy.69), calls=%async_computation.6 | async-start | bytes 1048576 | tf_op jit(solution)/shard_map/all_to_all | solution.py:152
  464.6 19.7 %all-to-all-start.8 = ((bf16[2,1024,128]{2,0,1:T(2,128)(2,1)}), bf16[2,1024,128]{2,0,1:T(2,128)(2,1)}, u32[]{:S(2)}, u32[]{:S(2)}) async-start(bf16[2,1024,128]{2,0,1:T(2,128)(2,1)} %copy.73), calls=%async_computation.8 | async-start | bytes 1048576 | tf_op jit(solution)/shard_map/all_to_all | solution.py:156
  606.9 24.2 %all-to-all-start.9 = ((bf16[2,128,1024]{1,0,2:T(2,128)(2,1)}), bf16[2,128,1024]{1,0,2:T(2,128)(2,1)}, u32[]{:S(2)}, u32[]{:S(2)}) async-start(bf16[2,128,1024]{1,0,2:T(2,128)(2,1)} %copy.75), calls=%async_computation.9 | async-start | bytes 1048576 | tf_op jit(solution)/shard_map/all_to_all | solution.py:235
  631.1 41.5 %all-to-all-start.13 = ((bf16[2,1024,128]{2,0,1:T(2,128)(2,1)}), bf16[2,1024,128]{2,0,1:T(2,128)(2,1)}, u32[]{:S(2)}, u32[]{:S(2)}) async-start(bf16[2,1024,128]{2,0,1:T(2,128)(2,1)} %copy.83), calls=%async_computation.13 | async-start | bytes 1048576 | tf_op jit(solution)/shard_map/all_to_all | solution.py:156
  672.6 20.6 %all-to-all-start.12 = ((bf16[2,1024,128]{2,0,1:T(2,128)(2,1)}), bf16[2,1024,128]{2,0,1:T(2,128)(2,1)}, u32[]{:S(2)}, u32[]{:S(2)}) async-start(bf16[2,1024,128]{2,0,1:T(2,128)(2,1)} %copy.81), calls=%async_computation.12 | async-start | bytes 1048576 | tf_op jit(solution)/shard_map/all_to_all | solution.py:242
  693.2 19.2 %all-to-all-start.11 = ((bf16[2,1024,128]{2,0,1:T(2,128)(2,1)}), bf16[2,1024,128]{2,0,1:T(2,128)(2,1)S(1)}, u32[]{:S(2)}, u32[]{:S(2)}) async-start(bf16[2,1024,128]{2,0,1:T(2,128)(2,1)} %copy.79), calls=%async_computation.11 | async-start | bytes 1048576 | tf_op jit(solution)/shard_map/all_to_all | solution.py:241
  712.4 20.6 %all-to-all-start.10 = ((bf16[2,1024,128]{2,0,1:T(2,128)(2,1)}), bf16[2,1024,128]{2,0,1:T(2,128)(2,1)S(1)}, u32[]{:S(2)}, u32[]{:S(2)}) async-start(bf16[2,1024,128]{2,0,1:T(2,128)(2,1)} %copy.77), calls=%async_computation.10 | async-start | bytes 1048576 | tf_op jit(solution)/shard_map/all_to_all | solution.py:240
  733.0 34.0 %all-to-all-start.7 = ((bf16[2,1024,128]{2,0,1:T(2,128)(2,1)}), bf16[2,1024,128]{2,0,1:T(2,128)(2,1)}, u32[]{:S(2)}, u32[]{:S(2)}) async-start(bf16[2,1024,128]{2,0,1:T(2,128)(2,1)} %copy.71), calls=%async_computation.7 | async-start | bytes 1048576 | tf_op jit(solution)/shard_map/all_to_all | solution.py:156
  767.1 20.7 %all-to-all-start.14 = ((bf16[2,128,1024]{1,0,2:T(2,128)(2,1)}), bf16[2,128,1024]{1,0,2:T(2,128)(2,1)S(1)}, u32[]{:S(2)}, u32[]{:S(2)}) async-start(bf16[2,128,1024]{1,0,2:T(2,128)(2,1)} %copy.85), calls=%async_computation.14 | async-start | bytes 1048576 | tf_op jit(solution)/shard_map/all_to_all | solution.py:235
  842.0 20.5 %all-to-all-start.15 = ((bf16[2,1024,128]{2,0,1:T(2,128)(2,1)}), bf16[2,1024,128]{2,0,1:T(2,128)(2,1)}, u32[]{:S(2)}, u32[]{:S(2)}) async-start(bf16[2,1024,128]{2,0,1:T(2,128)(2,1)} %copy.87), calls=%async_computation.15 | async-start | bytes 1048576 | tf_op jit(solution)/shard_map/all_to_all | solution.py:240
  862.5 20.6 %all-to-all-start.16 = ((bf16[2,1024,128]{2,0,1:T(2,128)(2,1)}), bf16[2,1024,128]{2,0,1:T(2,128)(2,1)S(1)}, u32[]{:S(2)}, u32[]{:S(2)}) async-start(bf16[2,1024,128]{2,0,1:T(2,128)(2,1)} %copy.89), calls=%async_computation.16 | async-start | bytes 1048576 | tf_op jit(solution)/shard_map/all_to_all | solution.py:241
  867.7 147.6 %all-reduce.3.cloned.1.call-start = ((), (), s32[]{:S(2)}) async-start(), calls=%async_computation.26 | async-start | bytes 262144 | tf_op jit(solution)/shard_map/psum | solution.py:38
  (132 other events, 4707.4 us)
Sparse Core Ops, SparseCore 0:
  11.1 72.8 all-gather.16
  85.9 35.3 all-gather.18
  123.2 87.5 all-gather.22
  212.5 87.5 all-gather.20
  301.8 70.1 all-gather.24
  373.7 35.6 all-gather.26
  411.3 87.5 all-gather.28
  500.8 87.6 all-gather.30
  894.6 120.6 all-reduce.2
where the time goes:
time: 1030 us
  waiting for transfers between devices  582 us (57%)
  matrix products  183 us (18%)
  local copies, waits for them, and re-layouts  114 us (11%)
  starting transfers between devices  79.7 us (8%)
  other arithmetic  48.3 us (5%)
  between operations  16 us (2%)
    psum x1, waiting for transfers between devices, sum_adapters(): return lax.psum((down_terms, up_terms), ('dp', 'sp'))  118 us
    all_gather x2, waiting for transfers between devices, fetch_weights(): lax.all_gather(query_key_value_weight[layer_number], 'dp', axis=0, tiled=...  118 us
    all_gather x2, waiting for transfers between devices, fetch_weights(): lax.all_gather(feedforward_out_weight[layer_number], 'dp', axis=0, tiled=...  104 us
    all_gather x2, waiting for transfers between devices, fetch_weights(): lax.all_gather(feedforward_in_weight[layer_number], 'dp', axis=0, tiled=T...  96 us
    all_to_all x4, waiting for transfers between devices, layer_forward(): lax.all_to_all(mixture_h, 'sp', split_axis=1, concat_axis=2, tiled=True)  30 us
    dot_general x2, matrix products, layer_backward(): jnp.einsum('stf,df->std', grad_pre, feedforward_in_weight, preferred_elem...  24.1 us
    all_to_all x2, waiting for transfers between devices, layer_forward(): lax.all_to_all(query_rows, 'sp', split_axis=2, concat_axis=1, tiled=True)  24.1 us
    dot_general x2, matrix products, layer_forward(): jnp.einsum('stf,fd->std', activation, feedforward_out_weight, preferred_e...  23.5 us
  transfers between devices with their start and end apart: 27, of which 20 were waited for; matrix products, arithmetic and copies ran while one was open for 24% of the time, Pallas kernels for 0%

commit v1 on v0

--- a/solution.py
+++ b/solution.py
@@ -10,6 +10,28 @@
 ADAPTER_ALPHA = 32.0
 EXACT_PRECISION = lax.Precision.HIGHEST
 MASKED = -1e30
+
+
+def split_up(x, dim, peers):
+    before, after = (x.shape[:dim], x.shape[dim + 1 :])
+    return jnp.moveaxis(x.reshape(*before, peers, -1, *after), dim, 0)
+
+
+def in_order(blocks, dim):
+    blocks = jnp.moveaxis(blocks, 0, dim)
+    shape = blocks.shape
+    return blocks.reshape(*shape[:dim], shape[dim] * shape[dim + 1], *shape[dim + 2 :])
+
+
+def sent_to_each(x, axis, split_dim, concat_dim):
+    count, position = (lax.axis_size(axis), lax.axis_index(axis))
+    parts = split_up(x, split_dim, count)
+    finished = [parts[position]]
+    for hop in range(1, count):
+        sent = parts[(position + hop) % count]
+        finished.append(lax.ppermute(sent, axis, [(i, (i + hop) % count) for i in range(count)]))
+    parts = jnp.stack(finished)[(position - jnp.arange(count)) % count]
+    return in_order(parts, concat_dim)
 
 
 def layer_norm(tensor, gains, shifts):
@@ -150,7 +172,7 @@
     queries_h, keys_h, values_h = (
         lax.all_to_all(query_rows, "sp", split_axis=2, concat_axis=1, tiled=True),
         lax.all_to_all(key_rows, "sp", split_axis=2, concat_axis=1, tiled=True),
-        lax.all_to_all(value_rows, "sp", split_axis=2, concat_axis=1, tiled=True),
+        sent_to_each(value_rows, "sp", 2, 1),
     )
     mixture_h, log_total = lax.map(slot_forward, (queries_h, keys_h, values_h, document_begin))
     mixture = lax.all_to_all(mixture_h, "sp", split_axis=1, concat_axis=2, tiled=True)

time: 1030 us -> 1030 us (level)
  waiting for transfers between devices: 582 us -> 555 us
  starting transfers between devices: 79.7 us -> 93.7 us
  local copies, waits for them, and re-layouts: 114 us -> 126 us
    all_to_all x2 -> x0, waiting for transfers between devices: 22.2 us -> none  [layer_forward(): lax.all_to_all(value_rows, 'sp', split_axis=2, concat_axis=1, tiled=True)]
    all_to_all x2, waiting for transfers between devices: 24.1 us -> 5.95 us  [layer_forward(): lax.all_to_all(query_rows, 'sp', split_axis=2, concat_axis=1, tiled=True)]
    ppermute x0 -> x14, starting transfers between devices: none -> 17.8 us  [sent_to_each(): lax.ppermute(sent, axis, [(i, (i + hop) % count) for i in range(count)])]
    all_gather x2, waiting for transfers between devices: 96 us -> 107 us  [fetch_weights(): lax.all_gather(feedforward_in_weight[layer_number], 'dp', axis=0, tiled=T...]
  transfers between devices with their start and end apart: 27 -> 39, of which waited for: 20 -> 20; matrix products, arithmetic and copies ran while one was open for 24% -> 26% of each run, Pallas kernels for 0% -> 0%
where the time goes in v1:
time: 1030 us; the launch traced here: 1020 us
  waiting for transfers between devices  555 us (54%)
  matrix products  183 us (18%)
  local copies, waits for them, and re-layouts  126 us (12%)
  starting transfers between devices  93.7 us (9%)
  other arithmetic  48.9 us (5%)
  between operations  16 us (2%)
    psum x1, waiting for transfers between devices, sum_adapters(): return lax.psum((down_terms, up_terms), ('dp', 'sp'))  118 us
    all_gather x2, waiting for transfers between devices, fetch_weights(): lax.all_gather(feedforward_out_weight[layer_number], 'dp', axis=0, tiled=...  114 us
    all_gather x2, waiting for transfers between devices, fetch_weights(): lax.all_gather(query_key_value_weight[layer_number], 'dp', axis=0, tiled=...  113 us
    all_gather x2, waiting for transfers between devices, fetch_weights(): lax.all_gather(feedforward_in_weight[layer_number], 'dp', axis=0, tiled=T...  107 us
    all_to_all x4, waiting for transfers between devices, layer_forward(): lax.all_to_all(mixture_h, 'sp', split_axis=1, concat_axis=2, tiled=True)  29.3 us
    dot_general x2, matrix products, layer_backward(): jnp.einsum('stf,df->std', grad_pre, feedforward_in_weight, preferred_elem...  24.1 us
    dot_general x2, matrix products, layer_forward(): jnp.einsum('stf,fd->std', activation, feedforward_out_weight, preferred_e...  23.5 us
  transfers between devices with their start and end apart: 39, of which 20 were waited for; matrix products, arithmetic and copies ran while one was open for 26% of the time, Pallas kernels for 0%

profile of v1, /device:TPU:0, one launch (start us, length us, event | category | flops | bytes accessed | tf_op | source)
XLA Modules:
  0.0 1024.5 jit_solution(18101502161913877222)
XLA Ops:
  29.6 54.6 %all-gather.17.cloned.1.call-done = bf16[1,1024,3072]{2,1,0:T(8,128)(2,1)} async-done(((bf16[1,256,3072]{2,1,0:T(8,128)(2,1)}), bf16[1,1024,3072]{2,1,0:T(8,128)(2,1)}) %all-gather.17.cloned.1.call-update) | async-done | bytes 6291472 | tf_op jit(solution)/shard_map/all_gather | solution.py:52
  126.4 13.5 %all-to-all-done.1 = bf16[2,128,1024]{1,0,2:T(2,128)(2,1)S(1)} async-done(((bf16[2,128,1024]{1,0,2:T(2,128)(2,1)}), bf16[2,128,1024]{1,0,2:T(2,128)(2,1)S(1)}, u32[]{:S(2)}, u32[]{:S(2)}) %all-to-all-start.1) | async-done | bytes 524320 | tf_op jit(solution)/shard_map/all_to_all | solution.py:174
  140.6 12.9 %while.72 = (s32[]{:T(128)}, bf16[2,1024,128]{1,2,0:T(8,128)(2,1)S(1)}, bf16[2,1024,128]{1,2,0:T(8,128)(2,1)S(1)}, s32[2,1024]{1,0:T(2,128)S(1)}, bf16[2,1024,12...) while((s32[]{:T(128)}, bf16[2,1024,128]{1,2,0:T(8,128)(2,1)S(1)}, ...), condition=%wide.region_5.6_spmd, body=%wide.region_2.5_spmd.sunk | while | flops 556922880 | bytes 32575588 | solution.py:177
  159.7 14.0 %all-to-all-done.2 = bf16[2,1024,128]{2,0,1:T(2,128)(2,1)S(1)} async-done(((bf16[2,1024,128]{2,0,1:T(2,128)(2,1)}), bf16[2,1024,128]{2,0,1:T(2,128)(2,1)S(1)}, u32[]{:S(2)}, u32[]{:S(2)}) %all-to-all-start.2) | async-done | bytes 524320 | tf_op jit(solution)/shard_map/all_to_all | solution.py:178
  177.9 32.9 %all-gather.23.cloned.1.call-done = bf16[1,4096,1024]{2,1,0:T(8,128)(2,1)} async-done(((bf16[1,1024,1024]{2,1,0:T(8,128)(2,1)}), bf16[1,4096,1024]{2,1,0:T(8,128)(2,1)}) %all-gather.23.cloned.1.call-update) | async-done | bytes 8388624 | tf_op jit(solution)/shard_map/all_gather | solution.py:55
  210.8 89.3 %all-gather.21.cloned.1.call-done = bf16[1,1024,4096]{2,1,0:T(8,128)(2,1)} async-done(((bf16[1,256,4096]{2,1,0:T(8,128)(2,1)}), bf16[1,1024,4096]{2,1,0:T(8,128)(2,1)}) %all-gather.21.cloned.1.call-update) | async-done | bytes 8388624 | tf_op jit(solution)/shard_map/all_gather | solution.py:54
  300.2 11.5 %fusion.341 = (f32[2,128]{1,0:T(2,128)S(1)}, f32[2,128,1024]{2,1,0:T(8,128)S(1)}) fusion(f32[2,128,1024]{2,1,0:T(8,128)} %copy-done.50, f32[1024]{0:T(1024)S(1)} %bitcast.832, bf16[1,4096,1024]{2,1,0:T(8,128)(2,1)} %all-gather.23.cloned.1.call-done, bf16[1,1024,4096]{2,1,0:T(8,128)(2,1)} %all-gather.21.cloned.1.call-done, f32[4096]{0:T(1024)S(1)} %bitcast.827, ...), kind=kOutput, calls=%fused_computation.482 | convolution fusion | flops 4307550208 | bytes 18906112 | tf_op jit(solution)/shard_map/stf,fd->std/dot_general | solution.py:192
  313.1 58.9 %all-gather.25.cloned.1.call-done = bf16[1,1024,3072]{2,1,0:T(8,128)(2,1)} async-done(((bf16[1,256,3072]{2,1,0:T(8,128)(2,1)}), bf16[1,1024,3072]{2,1,0:T(8,128)(2,1)}) %all-gather.25.cloned.1.call-update) | async-done | bytes 6291472 | tf_op jit(solution)/shard_map/all_gather | solution.py:52
  434.8 16.5 %while.74 = (s32[]{:T(128)}, bf16[2,1024,128]{1,2,0:T(8,128)(2,1)}, f32[2,2,1024]{2,1,0:T(2,128)S(1)}, bf16[2,1024,128]{1,2,0:T(8,128)(2,1)S(1)}, s32[2,1024]{1,...) while((s32[]{:T(128)}, bf16[2,1024,128]{1,2,0:T(8,128)(2,1)}, ...), condition=%wide.region_19.20_spmd, body=%wide.region_16.19_spmd.sunk | while | flops 556922880 | bytes 36778152 | solution.py:177
  458.0 15.3 %all-to-all-done.6 = bf16[2,1024,128]{2,0,1:T(2,128)(2,1)} async-done(((bf16[2,1024,128]{2,0,1:T(2,128)(2,1)}), bf16[2,1024,128]{2,0,1:T(2,128)(2,1)}, u32[]{:S(2)}, u32[]{:S(2)}) %all-to-all-start.6) | async-done | bytes 524320 | tf_op jit(solution)/shard_map/all_to_all | solution.py:178
  481.4 17.2 %all-gather.29.cloned.1.call-done = bf16[1,1024,4096]{2,1,0:T(8,128)(2,1)} async-done(((bf16[1,256,4096]{2,1,0:T(8,128)(2,1)}), bf16[1,1024,4096]{2,1,0:T(8,128)(2,1)}) %all-gather.29.cloned.1.call-update) | async-done | bytes 8388624 | tf_op jit(solution)/shard_map/all_gather | solution.py:54
  498.6 8.2 fusion.75
  506.7 81.3 %all-gather.31.cloned.1.call-done = bf16[1,4096,1024]{2,1,0:T(8,128)(2,1)} async-done(((bf16[1,1024,1024]{2,1,0:T(8,128)(2,1)}), bf16[1,4096,1024]{2,1,0:T(8,128)(2,1)}) %all-gather.31.cloned.1.call-update) | async-done | bytes 8388624 | tf_op jit(solution)/shard_map/all_gather | solution.py:55
  588.1 12.2 %multiply_reduce_fusion.5 = (f32[2,128]{1,0:T(2,128)S(1)}, f32[2,128,1024]{2,1,0:T(8,128)}) fusion(f32[2,128,1024]{2,1,0:T(8,128)S(1)} %copy-done.22, f32[2,128]{1,0:T(2,128)S(1)} %broadcast_multiply_fusion.5, f32[1024]{0:T(1024)S(1)} %bitcast.841, bf16[1,1024,4096]{2,1,0:T(8,128)(2,1)} %all-gather.29.cloned.1.call-done, f32[2,128,4096]{2,1,0:T(8,128)} %fusion.75, ...), kind=kOutput, calls=%fused_computation.281 | convolution fusion | flops 4316987392 | bytes 23599104 | tf_op jit(solution)/shard_map/stf,df->std/dot_general | solution.py:244
  612.6 15.4 %while.76 = (s32[]{:T(128)}, bf16[2,1024,128]{1,2,0:T(8,128)(2,1)}, f32[2,2,1024]{2,1,0:T(2,128)}, bf16[2,1024,128]{1,2,0:T(8,128)(2,1)S(1)}, s32[2,1024]{1,0:T(...) while((s32[]{:T(128)}, bf16[2,1024,128]{1,2,0:T(8,128)(2,1)}, ...), condition=%wide.region_32.33_spmd, body=%wide.region_29.32_spmd.sunk | while | flops 556922880 | bytes 32583792 | solution.py:177
  642.6 27.2 %while.75 = (s32[]{:T(128)}, bf16[2,1024,128]{1,2,0:T(8,128)(2,1)}, bf16[2,1024,128]{1,2,0:T(8,128)(2,1)}, bf16[2,1024,128]{1,2,0:T(8,128)(2,1)}, bf16[2,1024,12...) while((s32[]{:T(128)}, bf16[2,1024,128]{1,2,0:T(8,128)(2,1)}, ...), condition=%wide.region_26.27_spmd, body=%wide.region_24.26_spmd.sunk | while | flops 1370880000 | bytes 88150360 | solution.py:258
  715.0 12.9 %while.73 = (s32[]{:T(128)}, bf16[2,1024,128]{1,2,0:T(8,128)(2,1)S(1)}, bf16[2,1024,128]{1,2,0:T(8,128)(2,1)S(1)}, s32[2,1024]{1,0:T(2,128)S(1)}, bf16[2,1024,12...) while((s32[]{:T(128)}, bf16[2,1024,128]{1,2,0:T(8,128)(2,1)S(1)}, ...), condition=%wide.region_13.14_spmd, body=%wide.region_10.13_spmd.sunk | while | flops 556922880 | bytes 32575588 | solution.py:177
  748.2 11.9 %multiply_reduce_fusion.2 = (f32[2,128]{1,0:T(2,128)S(1)}, f32[2,128,1024]{2,1,0:T(8,128)}) fusion(f32[2,128,1024]{2,1,0:T(8,128)S(1)} %copy-done.29, f32[2,128]{1,0:T(2,128)S(1)} %broadcast_multiply_fusion.4, f32[1024]{0:T(1024)S(1)} %bitcast.845, bf16[1,1024,4096]{2,1,0:T(8,128)(2,1)} %all-gather.21.cloned.1.call-done, f32[2,128,4096]{2,1,0:T(8,128)} %fusion.69, ...), kind=kOutput, calls=%fused_computation.275 | convolution fusion | flops 4317249536 | bytes 24123392 | tf_op jit(solution)/shard_map/stf,df->std/dot_general | solution.py:244
  775.9 11.1 %all-to-all-done.12 = bf16[2,128,1024]{1,0,2:T(2,128)(2,1)S(1)} async-done(((bf16[2,128,1024]{1,0,2:T(2,128)(2,1)}), bf16[2,128,1024]{1,0,2:T(2,128)(2,1)S(1)}, u32[]{:S(2)}, u32[]{:S(2)}) %all-to-all-start.12) | async-done | bytes 524320 | tf_op jit(solution)/shard_map/all_to_all | solution.py:257
  791.9 28.5 %while.77 = (s32[]{:T(128)}, bf16[2,1024,128]{1,2,0:T(8,128)(2,1)}, bf16[2,1024,128]{1,2,0:T(8,128)(2,1)}, bf16[2,1024,128]{1,2,0:T(8,128)(2,1)}, bf16[2,1024,12...) while((s32[]{:T(128)}, bf16[2,1024,128]{1,2,0:T(8,128)(2,1)}, ...), condition=%wide.region_39.40_spmd, body=%wide.region_37.39_spmd.sunk | while | flops 1370880000 | bytes 86053176 | solution.py:258
  830.0 11.3 %all-to-all-done.15 = bf16[2,1024,128]{2,0,1:T(2,128)(2,1)S(1)} async-done(((bf16[2,1024,128]{2,0,1:T(2,128)(2,1)}), bf16[2,1024,128]{2,0,1:T(2,128)(2,1)S(1)}, u32[]{:S(2)}, u32[]{:S(2)}) %all-to-all-start.15) | async-done | bytes 524320 | tf_op jit(solution)/shard_map/all_to_all | solution.py:264
  845.8 12.0 %fusion.191 = f32[2,128,1024]{2,1,0:T(8,128)} fusion(f32[2,128,1024]{2,1,0:T(8,128)S(1)} %get-tuple-element.529, bf16[1,4096,1024]{2,1,0:T(8,128)(2,1)} %all-gather.31.cloned.1.call-done, bf16[1,1024,4096]{2,1,0:T(8,128)(2,1)} %all-gather.29.cloned.1.call-done, f32[4096]{0:T(1024)S(1)} %bitcast.826, f32[1024]{0:T(1024)S(1)} %bitcast.829, ...), kind=kOutput, calls=%fused_computation.235 | convolution fusion | flops 4307288064 | bytes 18905088 | tf_op jit(solution)/shard_map/stf,fd->std/dot_general | solution.py:192
  871.0 11.3 %all-to-all-done.14 = bf16[2,1024,128]{2,0,1:T(2,128)(2,1)S(1)} async-done(((bf16[2,1024,128]{2,0,1:T(2,128)(2,1)}), bf16[2,1024,128]{2,0,1:T(2,128)(2,1)S(1)}, u32[]{:S(2)}, u32[]{:S(2)}) %all-to-all-start.14) | async-done | bytes 524320 | tf_op jit(solution)/shard_map/all_to_all | solution.py:263
  896.4 118.3 %all-reduce.3.cloned.1.call-done = (f32[2,2,4,1024]{3,2,1,0:T(4,128)}, f32[2,2,4,1024]{3,2,1,0:T(4,128)}) async-done(((f32[2,2,4,1024]{3,2,1,0:T(4,128)}, f32[2,2,4,1024]{3,2,1,0:T(4,128)}), (f32[2,2,4,1024]{3,2,1,0:T(4,128)}, f32[2,2,4,1024]{3,2,1,0:T(4,128)})) %all-reduce.3.cloned.1.call-update) | async-done | bytes 131088 | tf_op jit(solution)/shard_map/psum | solution.py:60
  (659 shorter events, 422.5 us)
Async XLA Ops:
  7.2 77.0 %all-gather.17.cloned.1.call-start = ((), (), s32[]{:S(2)}) async-start(), calls=%async_computation.16 | async-start | bytes 7864320 | tf_op jit(solution)/shard_map/all_gather | solution.py:52
  11.1 163.9 %all-gather.19.cloned.1.call-start = ((), (), s32[]{:S(2)}) async-start(), calls=%async_computation.17 | async-start | bytes 2621440 | tf_op jit(solution)/shard_map/all_gather | solution.py:53
  12.3 198.5 %all-gather.23.cloned.1.call-start = ((), (), s32[]{:S(2)}) async-start(), calls=%async_computation.19 | async-start | bytes 10485760 | tf_op jit(solution)/shard_map/all_gather | solution.py:55
  17.0 283.2 %all-gather.21.cloned.1.call-start = ((), (), s32[]{:S(2)}) async-start(), calls=%async_computation.18 | async-start | bytes 10485760 | tf_op jit(solution)/shard_map/all_gather | solution.py:54
  21.9 350.1 %all-gather.25.cloned.1.call-start = ((), (), s32[]{:S(2)}) async-start(), calls=%async_computation.20 | async-start | bytes 7864320 | tf_op jit(solution)/shard_map/all_gather | solution.py:52
  22.5 455.0 %all-gather.27.cloned.1.call-start = ((), (), s32[]{:S(2)}) async-start(), calls=%async_computation.21 | async-start | bytes 2621440 | tf_op jit(solution)/shard_map/all_gather | solution.py:53
  23.1 475.5 %all-gather.29.cloned.1.call-start = ((), (), s32[]{:S(2)}) async-start(), calls=%async_computation.22 | async-start | bytes 10485760 | tf_op jit(solution)/shard_map/all_gather | solution.py:54
  23.9 564.2 %all-gather.31.cloned.1.call-start = ((), (), s32[]{:S(2)}) async-start(), calls=%async_computation.23 | async-start | bytes 10485760 | tf_op jit(solution)/shard_map/all_gather | solution.py:55
  92.7 26.1 %all-to-all-start = ((bf16[2,128,1024]{1,0,2:T(2,128)(2,1)}), bf16[2,128,1024]{1,0,2:T(2,128)(2,1)S(1)}, u32[]{:S(2)}, u32[]{:S(2)}) async-start(bf16[2,128,1024]{1,0,2:T(2,128)(2,1)} %copy.156), calls=%async_computation | async-start | bytes 1048576 | tf_op jit(solution)/shard_map/all_to_all | solution.py:173
  104.4 20.2 %collective-permute-start.2 = (bf16[2,128,128]{2,1,0:T(8,128)(2,1)S(1)}, bf16[2,128,128]{2,1,0:T(8,128)(2,1)S(1)}, u32[]{:S(2)}, u32[]{:S(2)}) collective-permute-start(bf16[2,128,128]{2,1,0:T(8,128)(2,1)S(1)} %bitcast.807), channel_id=1, source_target_pairs={{0,3},{1,4},{2,5},{3,6},{4,7},{5,0},{6,1},{7,2},{8,11},{9,12},{10,... | collective-permute-start | bytes 196616 | tf_op jit(solution)/shard_map/ppermute | solution.py:32
  118.8 21.1 %all-to-all-start.1 = ((bf16[2,128,1024]{1,0,2:T(2,128)(2,1)}), bf16[2,128,1024]{1,0,2:T(2,128)(2,1)S(1)}, u32[]{:S(2)}, u32[]{:S(2)}) async-start(bf16[2,128,1024]{1,0,2:T(2,128)(2,1)} %copy.158), calls=%async_computation.1 | async-start | bytes 1048576 | tf_op jit(solution)/shard_map/all_to_all | solution.py:174
  154.6 19.1 %all-to-all-start.2 = ((bf16[2,1024,128]{2,0,1:T(2,128)(2,1)}), bf16[2,1024,128]{2,0,1:T(2,128)(2,1)S(1)}, u32[]{:S(2)}, u32[]{:S(2)}) async-start(bf16[2,1024,128]{2,0,1:T(2,128)(2,1)} %copy.161), calls=%async_computation.2 | async-start | bytes 1048576 | tf_op jit(solution)/shard_map/all_to_all | solution.py:178
  382.2 26.3 %all-to-all-start.3 = ((bf16[2,128,1024]{1,0,2:T(2,128)(2,1)}), bf16[2,128,1024]{1,0,2:T(2,128)(2,1)}, u32[]{:S(2)}, u32[]{:S(2)}) async-start(bf16[2,128,1024]{1,0,2:T(2,128)(2,1)} %copy.172), calls=%async_computation.3 | async-start | bytes 1048576 | tf_op jit(solution)/shard_map/all_to_all | solution.py:173
  408.4 21.3 %all-to-all-start.4 = ((bf16[2,128,1024]{1,0,2:T(2,128)(2,1)}), bf16[2,128,1024]{1,0,2:T(2,128)(2,1)}, u32[]{:S(2)}, u32[]{:S(2)}) async-start(bf16[2,128,1024]{1,0,2:T(2,128)(2,1)} %copy.174), calls=%async_computation.4 | async-start | bytes 1048576 | tf_op jit(solution)/shard_map/all_to_all | solution.py:174
  453.4 19.9 %all-to-all-start.6 = ((bf16[2,1024,128]{2,0,1:T(2,128)(2,1)}), bf16[2,1024,128]{2,0,1:T(2,128)(2,1)}, u32[]{:S(2)}, u32[]{:S(2)}) async-start(bf16[2,1024,128]{2,0,1:T(2,128)(2,1)} %copy.180), calls=%async_computation.6 | async-start | bytes 1048576 | tf_op jit(solution)/shard_map/all_to_all | solution.py:178
  606.5 23.9 %all-to-all-start.7 = ((bf16[2,128,1024]{1,0,2:T(2,128)(2,1)}), bf16[2,128,1024]{1,0,2:T(2,128)(2,1)}, u32[]{:S(2)}, u32[]{:S(2)}) async-start(bf16[2,128,1024]{1,0,2:T(2,128)(2,1)} %copy.182), calls=%async_computation.7 | async-start | bytes 1048576 | tf_op jit(solution)/shard_map/all_to_all | solution.py:257
  630.4 41.5 %all-to-all-start.11 = ((bf16[2,1024,128]{2,0,1:T(2,128)(2,1)}), bf16[2,1024,128]{2,0,1:T(2,128)(2,1)}, u32[]{:S(2)}, u32[]{:S(2)}) async-start(bf16[2,1024,128]{2,0,1:T(2,128)(2,1)} %copy.192), calls=%async_computation.11 | async-start | bytes 1048576 | tf_op jit(solution)/shard_map/all_to_all | solution.py:178
  671.9 20.6 %all-to-all-start.10 = ((bf16[2,1024,128]{2,0,1:T(2,128)(2,1)}), bf16[2,1024,128]{2,0,1:T(2,128)(2,1)}, u32[]{:S(2)}, u32[]{:S(2)}) async-start(bf16[2,1024,128]{2,0,1:T(2,128)(2,1)} %copy.189), calls=%async_computation.10 | async-start | bytes 1048576 | tf_op jit(solution)/shard_map/all_to_all | solution.py:264
  711.4 20.6 %all-to-all-start.8 = ((bf16[2,1024,128]{2,0,1:T(2,128)(2,1)}), bf16[2,1024,128]{2,0,1:T(2,128)(2,1)S(1)}, u32[]{:S(2)}, u32[]{:S(2)}) async-start(bf16[2,1024,128]{2,0,1:T(2,128)(2,1)} %copy.185), calls=%async_computation.8 | async-start | bytes 1048576 | tf_op jit(solution)/shard_map/all_to_all | solution.py:262
  732.0 34.3 %all-to-all-start.5 = ((bf16[2,1024,128]{2,0,1:T(2,128)(2,1)}), bf16[2,1024,128]{2,0,1:T(2,128)(2,1)}, u32[]{:S(2)}, u32[]{:S(2)}) async-start(bf16[2,1024,128]{2,0,1:T(2,128)(2,1)} %copy.177), calls=%async_computation.5 | async-start | bytes 1048576 | tf_op jit(solution)/shard_map/all_to_all | solution.py:178
  766.3 20.6 %all-to-all-start.12 = ((bf16[2,128,1024]{1,0,2:T(2,128)(2,1)}), bf16[2,128,1024]{1,0,2:T(2,128)(2,1)S(1)}, u32[]{:S(2)}, u32[]{:S(2)}) async-start(bf16[2,128,1024]{1,0,2:T(2,128)(2,1)} %copy.194), calls=%async_computation.12 | async-start | bytes 1048576 | tf_op jit(solution)/shard_map/all_to_all | solution.py:257
  841.3 20.5 %all-to-all-start.13 = ((bf16[2,1024,128]{2,0,1:T(2,128)(2,1)}), bf16[2,1024,128]{2,0,1:T(2,128)(2,1)}, u32[]{:S(2)}, u32[]{:S(2)}) async-start(bf16[2,1024,128]{2,0,1:T(2,128)(2,1)} %copy.197), calls=%async_computation.13 | async-start | bytes 1048576 | tf_op jit(solution)/shard_map/all_to_all | solution.py:262
  861.8 20.6 %all-to-all-start.14 = ((bf16[2,1024,128]{2,0,1:T(2,128)(2,1)}), bf16[2,1024,128]{2,0,1:T(2,128)(2,1)S(1)}, u32[]{:S(2)}, u32[]{:S(2)}) async-start(bf16[2,1024,128]{2,0,1:T(2,128)(2,1)} %copy.199), calls=%async_computation.14 | async-start | bytes 1048576 | tf_op jit(solution)/shard_map/all_to_all | solution.py:263
  867.0 147.7 %all-reduce.3.cloned.1.call-start = ((), (), s32[]{:S(2)}) async-start(), calls=%async_computation.24 | async-start | bytes 262144 | tf_op jit(solution)/shard_map/psum | solution.py:60
  (146 other events, 3508.2 us)
Sparse Core Ops, SparseCore 0:
  11.2 72.8 all-gather.16
  86.0 35.3 all-gather.18
  123.2 87.5 all-gather.22
  212.5 87.5 all-gather.20
  301.8 70.1 all-gather.24
  373.7 35.3 all-gather.26
  410.9 87.5 all-gather.28
  500.4 87.5 all-gather.30
  893.9 120.7 all-reduce.2
